TPU v7x, 256 devices: a whole 4x4x8 slice. The times are simulated.
256 devices in a mesh: fsdp: 64 (over y, z, core), tensor: 4 (over x).
Axes of the slice: x: 4, y: 4, z: 8, core: 2. Of those that a mesh axis runs over, the one named last changes fastest.
Arguments:
- layer_input: bfloat16 [16384, 8192], P('fsdp', 'tensor'), may hold values from -6 to 6
- value_grad: bfloat16 [16384, 1024], P('fsdp', 'tensor'), may hold values from -6 to 6
- quant_codes: int32 [8192, 1024], P('fsdp', 'tensor'), may hold values from 0 to 15
- block_scales: float32 [8192, 16], P('fsdp', 'tensor'), may hold values from 0.02 to 0.08
- tenant_ids: int32 [1024], P('fsdp'), may hold values from 0 to 63
- live_counts: int32 [64], P('fsdp'), may hold values from 12 to 16, as said below
- tenant_owner: int32 [64], replicated, may hold values from 0 to 63, each once
- factor_down: float32 [64, 16, 8192], P('fsdp', None, 'tensor'), may hold values from -6 to 6
- factor_up: float32 [64, 16, 1024], P('fsdp', None, 'tensor'), may hold values from -6 to 6
- moment_down: float32 [64, 16, 8192], P('fsdp', None, 'tensor'), may hold values from -6 to 6
- second_down: float32 [64, 16, 8192], P('fsdp', None, 'tensor'), may hold values from 0.05 to 5
- moment_up: float32 [64, 16, 1024], P('fsdp', None, 'tensor'), may hold values from -6 to 6
- second_up: float32 [64, 16, 1024], P('fsdp', None, 'tensor'), may hold values from 0.05 to 5
Outputs:
- layer_input_gradient: bfloat16 [16384, 8192], P('fsdp', 'tensor')
- new_down: float32 [64, 16, 8192], P('fsdp', None, 'tensor')
- new_up: float32 [64, 16, 1024], P('fsdp', None, 'tensor')
- new_moment_down: float32 [64, 16, 8192], P('fsdp', None, 'tensor')
- new_second_down: float32 [64, 16, 8192], P('fsdp', None, 'tensor')
- new_moment_up: float32 [64, 16, 1024], P('fsdp', None, 'tensor')
- new_second_up: float32 [64, 16, 1024], P('fsdp', None, 'tensor')
Inputs may be any that keep to these rules, and one draw needn't show every extreme that they name: The first live_counts[f] sequence slots of fsdp index f are live and the rest are padding; some index has all 16 live. tenant_owner is a permutation: tenant t's adapter and its moments sit in slot tenant_owner[t].
All inputs are finite; a program needn't handle non-finite values.
Results may differ from a plain program's by a relative error of at most 0.01.
Values may be sent and summed in bfloat16 or wider, within the bound.
No kernel may reach another device: no remote copies, remote signals or barrier semaphores. Data moves between devices by JAX's collectives and lax.ppermute only.
A program may use at most 128 MiB of HBM per device.

v0:
```python
import math
import jax
import jax.numpy as jnp
from jax import lax
from jax.sharding import PartitionSpec as P

MODEL_WIDTH = 8192
ADAPTER_RANK = 16
nf4_levels = (
    -1.0,
    -0.6962,
    -0.5251,
    -0.3949,
    -0.2844,
    -0.1848,
    -0.0911,
    0.0,
    0.0796,
    0.1609,
    0.2461,
    0.3379,
    0.4407,
    0.5626,
    0.723,
    1.0,
)
adapter_scale = 2.0
beta_one = 0.9
beta_two = 0.999
adam_step = 10.0
learn_rate = 0.05
decay_rate = 0.01
adam_eps = 1e-08


def sent_together(arrays, axis, dim, along):
    ends, at = ([], 0)
    for a in arrays[:-1]:
        at += a.shape[along]
        ends.append(at)
    both = jnp.concatenate(arrays, axis=along)
    return tuple(jnp.split(lax.all_gather(both, axis, axis=dim, tiled=True), ends, axis=along))


def sent_to_all(x, axis):
    length = lax.axis_size(axis)
    return lax.all_to_all(jnp.broadcast_to(x[None], (length, *x.shape)), axis, 0, 0, tiled=True)


def over_copies(x, axis):
    return sent_to_all(x, axis).sum(axis=0)


def packed_total(arrays, axis):
    ends = [0]
    for a in arrays:
        ends.append(ends[-1] + a.size)
    total = over_copies(jnp.concatenate([a.ravel() for a in arrays]), axis)
    return tuple((total[b:e].reshape(a.shape) for a, b, e in zip(arrays, ends, ends[1:])))


def adam_update(param, grad, moment, second):
    new_moment = beta_one * moment + (1.0 - beta_one) * grad
    new_second = beta_two * second + (1.0 - beta_two) * grad * grad
    corrected = new_moment / (1.0 - beta_one**adam_step)
    divisor = jnp.sqrt(new_second / (1.0 - beta_two**adam_step)) + adam_eps
    new_param = param - learn_rate * (corrected / divisor + decay_rate * param)
    return (new_param, new_moment, new_second)


def dequantize(quant_codes, block_scales):
    levels_out = jnp.zeros(quant_codes.shape, jnp.float32)
    for position in range(16):
        levels_out = jnp.where(quant_codes == position, nf4_levels[position], levels_out)
    row_count, col_count = quant_codes.shape
    blocks = block_scales.shape[1]
    scaled = levels_out.reshape(row_count, blocks, col_count // blocks) * block_scales[:, :, None]
    return scaled.reshape(row_count, col_count).astype(jnp.bfloat16)


def right_product(left, right):
    return lax.dot_general(
        left, right, (((1,), (1,)), ((), ())), preferred_element_type=jnp.float32
    )


def left_product(left, right):
    return lax.dot_general(
        left, right, (((0,), (0,)), ((), ())), preferred_element_type=jnp.float32
    )


def add_sources(pieces):
    return (jnp.sum(pieces[0], axis=0, keepdims=True), jnp.sum(pieces[1], axis=0, keepdims=True))


def shards(
    layer_input,
    value_grad,
    quant_codes,
    block_scales,
    tenant_ids,
    live_counts,
    tenant_owner,
    factor_down,
    factor_up,
    moment_down,
    second_down,
    moment_up,
    second_up,
):
    tok_rows, width_part = layer_input.shape
    value_part = value_grad.shape[1]
    slot_count = tenant_ids.shape[0]
    seq_len = tok_rows // slot_count
    tenant_total = tenant_owner.shape[0]
    rank_size = factor_down.shape[1]
    inverse_width = 1.0 / math.sqrt(MODEL_WIDTH)
    coefficient = adapter_scale / math.sqrt(ADAPTER_RANK)
    live_seq = jnp.arange(slot_count, dtype=jnp.int32) < live_counts[0]
    live_tok = jnp.broadcast_to(live_seq[:, None], (slot_count, seq_len)).reshape(tok_rows)
    masked = jnp.where(live_tok[:, None], value_grad, jnp.zeros_like(value_grad))
    tenant_iota = jnp.arange(tenant_total, dtype=jnp.int32)
    matches = tenant_ids[:, None] == tenant_iota[None, :]
    slot_seq = jnp.sum(jnp.where(matches, tenant_owner[None, :], 0), axis=1)
    onehot_seq = (slot_seq[:, None] == tenant_iota[None, :]).astype(jnp.bfloat16)
    weight_local = dequantize(quant_codes, block_scales)
    all_down, all_up = sent_together(
        (factor_down.astype(jnp.bfloat16), factor_up.astype(jnp.bfloat16)), "fsdp", 0, 2
    )
    partial_value = right_product(masked, lax.all_gather(weight_local, "fsdp", axis=0, tiled=True))
    base_input_grad = lax.psum_scatter(
        partial_value.astype(jnp.bfloat16), "tensor", scatter_dimension=1, tiled=True
    ).astype(jnp.float32)
    flattened_down = all_down.reshape(tenant_total * rank_size, width_part)
    up_flat = all_up.reshape(tenant_total * rank_size, value_part)
    onehot_tok = jnp.broadcast_to(
        onehot_seq[:, None, :], (slot_count, seq_len, tenant_total)
    ).reshape(tok_rows, tenant_total)
    selector = onehot_tok.astype(jnp.float32)[:, :, None]
    down_scores = right_product(layer_input, flattened_down).reshape(
        tok_rows, tenant_total, rank_size
    )
    up_scores = right_product(masked, up_flat).reshape(tok_rows, tenant_total, rank_size)
    in_part = jnp.sum(down_scores * selector, axis=1) * inverse_width
    grad_part = jnp.sum(up_scores * selector, axis=1) * coefficient
    in_sum, grad_sum = packed_total((in_part, grad_part), "tensor")
    input_lowrank = in_sum.astype(jnp.bfloat16)
    gradient_lowrank = grad_sum.astype(jnp.bfloat16)
    spread_gradient = (onehot_tok[:, :, None] * gradient_lowrank[:, None, :]).reshape(
        tok_rows, tenant_total * rank_size
    )
    in_spread = (onehot_tok[:, :, None] * input_lowrank[:, None, :]).reshape(
        tok_rows, tenant_total * rank_size
    )
    adapter_input_grad = (
        jnp.dot(spread_gradient, flattened_down, preferred_element_type=jnp.float32) * inverse_width
    )
    down_terms = (left_product(spread_gradient, layer_input) * inverse_width).reshape(
        tenant_total, rank_size, width_part
    )
    up_terms = (left_product(in_spread, masked) * coefficient).reshape(
        tenant_total, rank_size, value_part
    )
    down_gradient, up_gradient = add_sources(
        (
            lax.all_to_all(
                down_terms.astype(jnp.bfloat16), "fsdp", split_axis=0, concat_axis=0, tiled=True
            ).astype(down_terms.dtype),
            lax.all_to_all(
                up_terms.astype(jnp.bfloat16), "fsdp", split_axis=0, concat_axis=0, tiled=True
            ).astype(up_terms.dtype),
        )
    )
    layer_input_gradient = (base_input_grad + adapter_input_grad).astype(jnp.bfloat16)
    new_down, new_moment_down, new_second_down = adam_update(
        factor_down, down_gradient, moment_down, second_down
    )
    new_up, new_moment_up, new_second_up = adam_update(factor_up, up_gradient, moment_up, second_up)
    return (
        layer_input_gradient,
        new_down,
        new_up,
        new_moment_down,
        new_second_down,
        new_moment_up,
        new_second_up,
    )


def solution(mesh):
    in_specs = (
        P("fsdp", "tensor"),
        P("fsdp", "tensor"),
        P("fsdp", "tensor"),
        P("fsdp", "tensor"),
        P("fsdp"),
        P("fsdp"),
        P(),
        P("fsdp", None, "tensor"),
        P("fsdp", None, "tensor"),
        P("fsdp", None, "tensor"),
        P("fsdp", None, "tensor"),
        P("fsdp", None, "tensor"),
        P("fsdp", None, "tensor"),
    )
    out_specs = (
        P("fsdp", "tensor"),
        P("fsdp", None, "tensor"),
        P("fsdp", None, "tensor"),
        P("fsdp", None, "tensor"),
        P("fsdp", None, "tensor"),
        P("fsdp", None, "tensor"),
        P("fsdp", None, "tensor"),
    )
    return jax.shard_map(shards, mesh=mesh, in_specs=in_specs, out_specs=out_specs, check_vma=False)
```

profile of v0, /device:TPU:1, one launch (start us, length us, event | category | flops | bytes accessed | tf_op | source)
XLA Modules:
  0.0 329.7 jit_solution(11363798175707540958)
XLA Ops:
  7.2 0.0 all-gather.3.cloned.1.call-start
  7.2 1.1 copy.97
  8.3 1.5 fusion.10
  9.8 0.0 all-gather.3.cloned.1.call-update
  9.8 0.0 all-gather.5.cloned.1.call-start
  9.9 0.7 convert_element_type.63
  10.6 0.9 convert_element_type.62
  11.5 0.6 pad_maximum_fusion
  12.1 0.0 all-gather.5.cloned.1.call-update
  12.1 0.0 reduce-scatter.2.cloned.1.call-start
  12.9 0.1 broadcast_in_dim.104
  12.9 0.1 broadcast_in_dim.105
  13.0 0.9 select_reduce_fusion
  13.9 0.1 fusion.13
  14.0 0.1 copy.114
  14.1 77.3 %all-gather.3.cloned.1.call-done = bf16[8192,256]{0,1:T(8,128)(2,1)} async-done(((bf16[128,256]{0,1:T(8,128)(2,1)}), bf16[8192,256]{0,1:T(8,128)(2,1)}) %all-gather.3.cloned.1.call-update) | async-done | bytes 4194320 | tf_op jit(solution)/shard_map/all_gather | solution.py:131
  91.3 5.6 %convolution_convert_fusion = bf16[256,8192]{1,0:T(8,128)(2,1)} fusion(bf16[8192,256]{0,1:T(8,128)(2,1)} %all-gather.3.cloned.1.call-done, bf16[256,256]{1,0:T(8,128)(2,1)} %param.14, pred[256]{0:T(512)(128)(4,1)S(1)} %broadcast_in_dim.105), kind=kOutput, calls=%fused_computation | convolution fusion | flops 1075904512 | bytes 8519936 | tf_op jit(solution)/shard_map/dot_general | solution.py:82
  97.0 76.3 %all-gather.5.cloned.1.call-done = bf16[64,16,2304]{2,1,0:T(8,128)(2,1)} async-done(((bf16[1,16,2304]{2,1,0:T(8,128)(2,1)}), bf16[64,16,2304]{2,1,0:T(8,128)(2,1)}) %all-gather.5.cloned.1.call-update) | async-done | bytes 4718608 | tf_op jit(solution)/shard_map/all_gather | solution.py:42
  173.3 1.1 split.9
  174.4 0.4 fusion.4
  174.8 2.2 slice-done
  177.0 1.3 fusion.20
  178.3 0.6 fusion.5
  178.9 0.1 copy.118
  179.0 0.1 mul.236
  179.1 0.1 copy.116
  179.2 0.1 mul.232
  179.3 0.7 broadcast_in_dim.127
  180.1 4.1 %all-to-all-start = ((f32[4,1,8192]{2,1,0:T(1,128)}), f32[4,1,8192]{2,1,0:T(1,128)S(1)}, u32[]{:S(2)}, u32[]{:S(2)}) async-start(f32[4,1,8192]{2,1,0:T(1,128)} %broadcast_in_dim.127), calls=%async_computation.1 | async-start | bytes 262144 | tf_op jit(solution)/shard_map/all_to_all | solution.py:47
  184.1 0.1 copy.113
  184.2 6.3 %all-to-all-done = f32[4,1,8192]{2,1,0:T(1,128)S(1)} async-done(((f32[4,1,8192]{2,1,0:T(1,128)}), f32[4,1,8192]{2,1,0:T(1,128)S(1)}, u32[]{:S(2)}, u32[]{:S(2)}) %all-to-all-start) | async-done | bytes 131104 | tf_op jit(solution)/shard_map/all_to_all | solution.py:47
  190.5 0.1 reduce_sum.61
  190.7 0.1 convert_element_type.65
  190.8 0.1 copy.120
  190.8 0.1 convert_element_type.70
  190.9 0.1 copy.121
  191.0 0.1 broadcast_multiply_fusion
  191.1 1.2 fusion.3
  192.3 7.4 %all-to-all-start.2 = ((bf16[64,16,256]{2,1,0:T(8,128)(2,1)}), bf16[64,16,256]{2,1,0:T(8,128)(2,1)S(1)}, u32[]{:S(2)}, u32[]{:S(2)}) async-start(bf16[64,16,256]{2,1,0:T(8,128)(2,1)} %bitcast.12), calls=%async_computation.3 | async-start | bytes 1048576 | tf_op jit(solution)/shard_map/all_to_all | solution.py:170
  199.7 3.2 multiply_convert_fusion
  202.9 14.1 %all-to-all-done.2 = bf16[64,16,256]{2,1,0:T(8,128)(2,1)S(1)} async-done(((bf16[64,16,256]{2,1,0:T(8,128)(2,1)}), bf16[64,16,256]{2,1,0:T(8,128)(2,1)S(1)}, u32[]{:S(2)}, u32[]{:S(2)}) %all-to-all-start.2) | async-done | bytes 524320 | tf_op jit(solution)/shard_map/all_to_all | solution.py:170
  217.0 6.6 %all-to-all-start.1 = ((bf16[64,16,2048]{2,1,0:T(8,128)(2,1)}), bf16[64,16,2048]{2,1,0:T(8,128)(2,1)}, u32[]{:S(2)}, u32[]{:S(2)}) async-start(bf16[64,16,2048]{2,1,0:T(8,128)(2,1)} %bitcast.48), calls=%async_computation.2 | async-start | bytes 8388608 | tf_op jit(solution)/shard_map/all_to_all | solution.py:167
  223.6 0.1 convert_reduce_fusion.1
  223.7 0.6 multiply_subtract_fusion.1
  224.4 4.7 %fusion.2 = bf16[256,2048]{1,0:T(8,128)(2,1)} fusion(bf16[256,2048]{1,0:T(8,128)(2,1)} %reduce-scatter.2.cloned.1.call-done, bf16[256,16]{0,1:T(8,128)(2,1)S(1)} %copy.120, bf16[256,64]{0,1:T(8,128)(2,1)S(1)} %copy.113, bf16[64,16,2304]{2,1,0:T(8,128)(2,1)} %all-gather.5.cloned.1.call-done), kind=kOutput, calls=%fused_computation.6 | convolution fusion | flops 1076101120 | bytes 6332416 | tf_op jit(solution)/shard_map/dot_general | solution.py:157
  229.1 90.3 %all-to-all-done.1 = bf16[64,16,2048]{2,1,0:T(8,128)(2,1)} async-done(((bf16[64,16,2048]{2,1,0:T(8,128)(2,1)}), bf16[64,16,2048]{2,1,0:T(8,128)(2,1)}, u32[]{:S(2)}, u32[]{:S(2)}) %all-to-all-start.1) | async-done | bytes 4194336 | tf_op jit(solution)/shard_map/all_to_all | solution.py:167
  319.5 2.9 convert_reduce_fusion
  322.4 0.8 multiply_subtract_fusion
  (26 shorter events, 0.1 us)
Async XLA Ops:
  7.2 167.7 %copy-start = (bf16[256,2048]{1,0:T(8,128)(2,1)S(1)}, bf16[256,2048]{1,0:T(8,128)(2,1)}, u32[]{:S(2)}) copy-start(bf16[256,2048]{1,0:T(8,128)(2,1)} %param.13) | copy-start | bytes 3145732
  7.2 84.2 %all-gather.3.cloned.1.call-start = ((), (), s32[]{:S(2)}) async-start(), calls=%async_computation.4 | async-start | bytes 4259840 | tf_op jit(solution)/shard_map/all_gather | solution.py:131
  9.8 163.5 %all-gather.5.cloned.1.call-start = ((), (), s32[]{:S(2)}) async-start(), calls=%async_computation.6 | async-start | bytes 4792320 | tf_op jit(solution)/shard_map/all_gather | solution.py:42
  12.1 212.2 %reduce-scatter.2.cloned.1.call-start = ((), (), s32[]{:S(2)}) async-start(), calls=%async_computation.5 | async-start | bytes 5242880 | tf_op jit(solution)/shard_map/reduce_scatter | solution.py:132
  96.9 77.4 %copy-start.2 = (bf16[256,256]{1,0:T(8,128)(2,1)S(1)}, bf16[256,256]{1,0:T(8,128)(2,1)}, u32[]{:S(2)}) copy-start(bf16[256,256]{1,0:T(8,128)(2,1)} %param.14) | copy-start | bytes 393220
  174.8 2.2 slice-start
  180.1 10.4 %all-to-all-start = ((f32[4,1,8192]{2,1,0:T(1,128)}), f32[4,1,8192]{2,1,0:T(1,128)S(1)}, u32[]{:S(2)}, u32[]{:S(2)}) async-start(f32[4,1,8192]{2,1,0:T(1,128)} %broadcast_in_dim.127), calls=%async_computation.1 | async-start | bytes 262144 | tf_op jit(solution)/shard_map/all_to_all | solution.py:47
  192.3 24.7 %all-to-all-start.2 = ((bf16[64,16,256]{2,1,0:T(8,128)(2,1)}), bf16[64,16,256]{2,1,0:T(8,128)(2,1)S(1)}, u32[]{:S(2)}, u32[]{:S(2)}) async-start(bf16[64,16,256]{2,1,0:T(8,128)(2,1)} %bitcast.12), calls=%async_computation.3 | async-start | bytes 1048576 | tf_op jit(solution)/shard_map/all_to_all | solution.py:170
  217.0 6.7 %copy-start.5 = (f32[1,16,256]{2,1,0:T(8,128)S(1)}, f32[1,16,256]{2,1,0:T(8,128)}, u32[]{:S(2)}) copy-start(f32[1,16,256]{2,1,0:T(8,128)} %param.21) | copy-start | bytes 49156
  217.0 6.7 %copy-start.6 = (f32[1,16,256]{2,1,0:T(8,128)S(1)}, f32[1,16,256]{2,1,0:T(8,128)}, u32[]{:S(2)}) copy-start(f32[1,16,256]{2,1,0:T(8,128)} %param.24) | copy-start | bytes 49156
  217.0 6.7 %copy-start.7 = (f32[1,16,256]{2,1,0:T(8,128)S(1)}, f32[1,16,256]{2,1,0:T(8,128)}, u32[]{:S(2)}) copy-start(f32[1,16,256]{2,1,0:T(8,128)} %param.25) | copy-start | bytes 49156
  217.0 102.5 %all-to-all-start.1 = ((bf16[64,16,2048]{2,1,0:T(8,128)(2,1)}), bf16[64,16,2048]{2,1,0:T(8,128)(2,1)}, u32[]{:S(2)}, u32[]{:S(2)}) async-start(bf16[64,16,2048]{2,1,0:T(8,128)(2,1)} %bitcast.48), calls=%async_computation.2 | async-start | bytes 8388608 | tf_op jit(solution)/shard_map/all_to_all | solution.py:167
  229.1 93.2 %copy-start.1 = (f32[1,16,2048]{2,1,0:T(8,128)S(1)}, f32[1,16,2048]{2,1,0:T(8,128)}, u32[]{:S(2)}) copy-start(f32[1,16,2048]{2,1,0:T(8,128)} %param.20) | copy-start | bytes 393220
  229.1 93.2 %copy-start.3 = (f32[1,16,2048]{2,1,0:T(8,128)S(1)}, f32[1,16,2048]{2,1,0:T(8,128)}, u32[]{:S(2)}) copy-start(f32[1,16,2048]{2,1,0:T(8,128)} %param.22) | copy-start | bytes 393220
  229.1 93.2 %copy-start.4 = (f32[1,16,2048]{2,1,0:T(8,128)S(1)}, f32[1,16,2048]{2,1,0:T(8,128)}, u32[]{:S(2)}) copy-start(f32[1,16,2048]{2,1,0:T(8,128)} %param.23) | copy-start | bytes 393220
Sparse Core Ops, SparseCore 0:
  11.1 80.1 all-gather.2
  94.7 78.5 all-gather.4
  175.8 47.7 reduce-scatter.1
where the time goes:
time: 330 us
  waiting for transfers between devices  264 us (80%)
  starting transfers between devices  18.2 us (6%)
  matrix products  16.4 us (5%)
  between operations  14.6 us (4%)
  other arithmetic  9.92 us (3%)
  local copies, waits for them, and re-layouts  6.16 us (2%)
    all_to_all x1, waiting for transfers between devices, shards(): lax.all_to_all(down_terms.astype(jnp.bfloat16), 'fsdp', split_axis=0, con...  90.3 us
    all_gather x1, waiting for transfers between devices, shards(): lax.all_gather(weight_local, 'fsdp', axis=0, tiled=True)  77.3 us
    all_gather x1, waiting for transfers between devices, sent_together(): lax.all_gather(both, axis, axis=dim, tiled=True)  76.3 us
    all_to_all x1, waiting for transfers between devices, shards(): lax.all_to_all(up_terms.astype(jnp.bfloat16), 'fsdp', split_axis=0, conca...  14.1 us
    all_to_all x1, starting transfers between devices, shards(): lax.all_to_all(up_terms.astype(jnp.bfloat16), 'fsdp', split_axis=0, conca...  7.43 us
    dot_general x3, matrix products, right_product(): lax.dot_general(left, right, (((1,), (1,)), ((), ())), preferred_element_...  7.3 us
    all_to_all x1, starting transfers between devices, shards(): lax.all_to_all(down_terms.astype(jnp.bfloat16), 'fsdp', split_axis=0, con...  6.61 us
  transfers between devices with their start and end apart: 6, of which 5 were waited for; matrix products, arithmetic and copies ran while one was open for 7% of the time, Pallas kernels for 0%

commit v1 on v0

--- a/solution.py
+++ b/solution.py
@@ -1,3 +1,4 @@
+import functools
 import math
 import jax
 import jax.numpy as jnp
@@ -31,6 +32,17 @@
 learn_rate = 0.05
 decay_rate = 0.01
 adam_eps = 1e-08
+
+
+def switch_lots_all_by_axis(inputs, mesh_ax):
+    side_arr = jnp.stack(lax.axis_size(mesh_ax) * [inputs], axis=0)
+    step_out = jnp.concatenate(
+        lax.all_to_all(side_arr, concat_axis=0, split_axis=0, axis_name=mesh_ax), axis=0
+    )
+    return step_out
+
+
+cut_corner = functools.partial(switch_lots_all_by_axis, mesh_ax="fsdp")
 
 
 def sent_together(arrays, axis, dim, along):
@@ -128,7 +140,7 @@
     all_down, all_up = sent_together(
         (factor_down.astype(jnp.bfloat16), factor_up.astype(jnp.bfloat16)), "fsdp", 0, 2
     )
-    partial_value = right_product(masked, lax.all_gather(weight_local, "fsdp", axis=0, tiled=True))
+    partial_value = right_product(masked, cut_corner(weight_local))
     base_input_grad = lax.psum_scatter(
         partial_value.astype(jnp.bfloat16), "tensor", scatter_dimension=1, tiled=True
     ).astype(jnp.float32)

time: 330 us -> 301 us (0.912)
  waiting for transfers between devices: 264 us -> 220 us
  starting transfers between devices: 18.2 us -> 30.3 us
    all_to_all x0 -> x1, waiting for transfers between devices: none -> 108 us  [switch_lots_all_by_axis(): lax.all_to_all(side_arr, concat_axis=0, split_axis=0, axis_name=mesh_ax)]
    all_gather x1 -> x0, waiting for transfers between devices: 77.3 us -> none  [shards(): lax.all_gather(weight_local, 'fsdp', axis=0, tiled=True)]
    all_gather x1, waiting for transfers between devices: 76.3 us -> 0.02 us  [sent_together(): lax.all_gather(both, axis, axis=dim, tiled=True)]
    all_to_all x0 -> x1, starting transfers between devices: none -> 13.5 us  [switch_lots_all_by_axis(): lax.all_to_all(side_arr, concat_axis=0, split_axis=0, axis_name=mesh_ax)]
  transfers between devices with their start and end apart: 6 -> 6, of which waited for: 5 -> 4; matrix products, arithmetic and copies ran while one was open for 7% -> 8% of each run, Pallas kernels for 0% -> 0%
where the time goes in v1:
time: 301 us; the launch traced here: 300 us
  waiting for transfers between devices  220 us (73%)
  starting transfers between devices  30.3 us (10%)
  between operations  16.4 us (5%)
  matrix products  16.3 us (5%)
  local copies, waits for them, and re-layouts  8.72 us (3%)
  other arithmetic  8.69 us (3%)
    all_to_all x1, waiting for transfers between devices, switch_lots_all_by_axis(): lax.all_to_all(side_arr, concat_axis=0, split_axis=0, axis_name=mesh_ax)  108 us
    all_to_all x1, waiting for transfers between devices, shards(): lax.all_to_all(down_terms.astype(jnp.bfloat16), 'fsdp', split_axis=0, con...  90.3 us
    all_to_all x1, waiting for transfers between devices, shards(): lax.all_to_all(up_terms.astype(jnp.bfloat16), 'fsdp', split_axis=0, conca...  14.1 us
    all_to_all x1, starting transfers between devices, switch_lots_all_by_axis(): lax.all_to_all(side_arr, concat_axis=0, split_axis=0, axis_name=mesh_ax)  13.5 us
    dot_general x3, matrix products, right_product(): lax.dot_general(left, right, (((1,), (1,)), ((), ())), preferred_element_...  7.22 us
    all_to_all x1, waiting for transfers between devices, sent_to_all(): lax.all_to_all(jnp.broadcast_to(x[None], (length, *x.shape)), axis, 0, 0,...  6.96 us
    all_to_all x1, starting transfers between devices, shards(): lax.all_to_all(down_terms.astype(jnp.bfloat16), 'fsdp', split_axis=0, con...  6.61 us
    all_to_all x1, starting transfers between devices, shards(): lax.all_to_all(up_terms.astype(jnp.bfloat16), 'fsdp', split_axis=0, conca...  6.13 us
  transfers between devices with their start and end apart: 6, of which 4 were waited for; matrix products, arithmetic and copies ran while one was open for 8% of the time, Pallas kernels for 0%

profile of v1, /device:TPU:1, one launch (start us, length us, event | category | flops | bytes accessed | tf_op | source)
XLA Modules:
  0.0 300.3 jit_solution(17583600548639113353)
XLA Ops:
  8.0 0.0 all-gather.2.cloned.1.call-start
  8.1 0.8 convert_element_type.63
  8.9 0.9 convert_element_type.62
  9.8 0.6 pad_maximum_fusion
  10.4 1.0 copy.100
  11.4 0.8 fusion.10
  12.3 0.1 copy.116
  12.4 2.5 stack.2
  14.9 13.5 %all-to-all-start = ((bf16[64,128,256]{2,1,0:T(8,128)(2,1)}), bf16[64,128,256]{2,1,0:T(8,128)(2,1)}, u32[]{:S(2)}, u32[]{:S(2)}) async-start(bf16[64,128,256]{2,1,0:T(8,128)(2,1)} %stack.2), calls=%async_computation | async-start | bytes 8388608 | tf_op jit(solution)/shard_map/all_to_all | solution.py:40
  28.4 0.0 reduce-scatter.2.cloned.1.call-start
  29.1 0.1 broadcast_in_dim.104
  29.2 0.1 broadcast_in_dim.105
  29.3 0.2 select_reduce_fusion
  29.5 0.1 fusion.13
  29.6 0.1 copy.118
  29.6 108.4 %all-to-all-done = bf16[64,128,256]{2,1,0:T(8,128)(2,1)} async-done(((bf16[64,128,256]{2,1,0:T(8,128)(2,1)}), bf16[64,128,256]{2,1,0:T(8,128)(2,1)}, u32[]{:S(2)}, u32[]{:S(2)}) %all-to-all-start) | async-done | bytes 4194336 | tf_op jit(solution)/shard_map/all_to_all | solution.py:40
  138.1 5.5 %convolution_convert_fusion = bf16[256,8192]{1,0:T(8,128)(2,1)} fusion(bf16[8192,256]{1,0:T(8,128)(2,1)} %bitcast.2, bf16[256,256]{1,0:T(8,128)(2,1)S(1)} %copy-done.2, pred[256]{0:T(512)(128)(4,1)S(1)} %broadcast_in_dim.105), kind=kOutput, calls=%fused_computation | convolution fusion | flops 1075904512 | bytes 8519936 | tf_op jit(solution)/shard_map/dot_general | solution.py:94
  143.6 0.0 all-gather.2.cloned.1.call-done
  143.6 1.1 split.9
  144.7 0.4 fusion.4
  145.2 2.2 slice-done
  147.4 1.3 fusion.20
  148.7 0.6 fusion.5
  149.3 0.1 copy.122
  149.4 0.1 mul.236
  149.5 0.1 copy.120
  149.6 0.1 mul.232
  149.7 0.7 broadcast_in_dim.127
  150.4 4.0 %all-to-all-start.1 = ((f32[4,1,8192]{2,1,0:T(1,128)}), f32[4,1,8192]{2,1,0:T(1,128)S(1)}, u32[]{:S(2)}, u32[]{:S(2)}) async-start(f32[4,1,8192]{2,1,0:T(1,128)} %broadcast_in_dim.127), calls=%async_computation.2 | async-start | bytes 262144 | tf_op jit(solution)/shard_map/all_to_all | solution.py:59
  154.4 0.1 copy.117
  154.5 7.0 %all-to-all-done.1 = f32[4,1,8192]{2,1,0:T(1,128)S(1)} async-done(((f32[4,1,8192]{2,1,0:T(1,128)}), f32[4,1,8192]{2,1,0:T(1,128)S(1)}, u32[]{:S(2)}, u32[]{:S(2)}) %all-to-all-start.1) | async-done | bytes 131104 | tf_op jit(solution)/shard_map/all_to_all | solution.py:59
  161.5 0.1 reduce_sum.61
  161.6 0.1 convert_element_type.65
  161.7 0.1 copy.124
  161.8 0.1 convert_element_type.70
  161.9 0.1 copy.125
  162.0 0.1 broadcast_multiply_fusion
  162.1 1.2 fusion.3
  163.3 6.1 %all-to-all-start.3 = ((bf16[64,16,256]{2,1,0:T(8,128)(2,1)}), bf16[64,16,256]{2,1,0:T(8,128)(2,1)S(1)}, u32[]{:S(2)}, u32[]{:S(2)}) async-start(bf16[64,16,256]{2,1,0:T(8,128)(2,1)} %bitcast.13), calls=%async_computation.4 | async-start | bytes 1048576 | tf_op jit(solution)/shard_map/all_to_all | solution.py:182
  169.4 3.2 %multiply_convert_fusion = bf16[1024,2048]{1,0:T(8,128)(2,1)} fusion(bf16[256,1024]{0,1:T(8,128)(2,1)S(1)} %bitcast.51, bf16[256,2048]{1,0:T(8,128)(2,1)S(1)} %copy-done), kind=kOutput, calls=%fused_computation.2 | convolution fusion | flops 1077936128 | bytes 5767168 | tf_op jit(solution)/shard_map/dot_general | solution.py:100
  172.6 14.1 %all-to-all-done.3 = bf16[64,16,256]{2,1,0:T(8,128)(2,1)S(1)} async-done(((bf16[64,16,256]{2,1,0:T(8,128)(2,1)}), bf16[64,16,256]{2,1,0:T(8,128)(2,1)S(1)}, u32[]{:S(2)}, u32[]{:S(2)}) %all-to-all-start.3) | async-done | bytes 524320 | tf_op jit(solution)/shard_map/all_to_all | solution.py:182
  186.7 6.6 %all-to-all-start.2 = ((bf16[64,16,2048]{2,1,0:T(8,128)(2,1)}), bf16[64,16,2048]{2,1,0:T(8,128)(2,1)}, u32[]{:S(2)}, u32[]{:S(2)}) async-start(bf16[64,16,2048]{2,1,0:T(8,128)(2,1)} %bitcast.49), calls=%async_computation.3 | async-start | bytes 8388608 | tf_op jit(solution)/shard_map/all_to_all | solution.py:179
  193.3 0.1 convert_reduce_fusion.1
  193.4 0.6 multiply_subtract_fusion.1
  194.1 4.7 %fusion.2 = bf16[256,2048]{1,0:T(8,128)(2,1)} fusion(bf16[256,2048]{1,0:T(8,128)(2,1)} %reduce-scatter.2.cloned.1.call-done, bf16[256,16]{0,1:T(8,128)(2,1)S(1)} %copy.124, bf16[256,64]{0,1:T(8,128)(2,1)S(1)} %copy.117, bf16[64,16,2304]{2,1,0:T(8,128)(2,1)} %all-gather.2.cloned.1.call-done), kind=kOutput, calls=%fused_computation.6 | convolution fusion | flops 1076101120 | bytes 6332416 | tf_op jit(solution)/shard_map/dot_general | solution.py:169
  198.8 90.3 %all-to-all-done.2 = bf16[64,16,2048]{2,1,0:T(8,128)(2,1)} async-done(((bf16[64,16,2048]{2,1,0:T(8,128)(2,1)}), bf16[64,16,2048]{2,1,0:T(8,128)(2,1)}, u32[]{:S(2)}, u32[]{:S(2)}) %all-to-all-start.2) | async-done | bytes 4194336 | tf_op jit(solution)/shard_map/all_to_all | solution.py:179
  289.2 2.9 convert_reduce_fusion
  292.1 0.8 multiply_subtract_fusion
  (31 shorter events, 0.1 us)
Async XLA Ops:
  8.0 137.2 %copy-start = (bf16[256,2048]{1,0:T(8,128)(2,1)S(1)}, bf16[256,2048]{1,0:T(8,128)(2,1)}, u32[]{:S(2)}) copy-start(bf16[256,2048]{1,0:T(8,128)(2,1)} %param.13) | copy-start | bytes 3145732
  8.0 135.6 %all-gather.2.cloned.1.call-start = ((), (), s32[]{:S(2)}) async-start(), calls=%async_computation.6 | async-start | bytes 4792320 | tf_op jit(solution)/shard_map/all_gather | solution.py:54
  14.9 14.4 %copy-start.8 = (s32[64]{0:T(128)S(1)}, s32[64]{0:T(128)}, u32[]{:S(2)}) copy-start(s32[64]{0:T(128)} %param.19) | copy-start | bytes 772
  14.9 14.4 %copy-start.9 = (s32[16]{0:T(128)S(1)}, s32[16]{0:T(128)}, u32[]{:S(2)}) copy-start(s32[16]{0:T(128)} %param.17) | copy-start | bytes 196
  14.9 123.2 %copy-start.2 = (bf16[256,256]{1,0:T(8,128)(2,1)S(1)}, bf16[256,256]{1,0:T(8,128)(2,1)}, u32[]{:S(2)}) copy-start(bf16[256,256]{1,0:T(8,128)(2,1)} %param.14) | copy-start | bytes 393220
  14.9 123.2 %all-to-all-start = ((bf16[64,128,256]{2,1,0:T(8,128)(2,1)}), bf16[64,128,256]{2,1,0:T(8,128)(2,1)}, u32[]{:S(2)}, u32[]{:S(2)}) async-start(bf16[64,128,256]{2,1,0:T(8,128)(2,1)} %stack.2), calls=%async_computation | async-start | bytes 8388608 | tf_op jit(solution)/shard_map/all_to_all | solution.py:40
  28.4 165.7 %reduce-scatter.2.cloned.1.call-start = ((), (), s32[]{:S(2)}) async-start(), calls=%async_computation.5 | async-start | bytes 5242880 | tf_op jit(solution)/shard_map/reduce_scatter | solution.py:144
  145.2 2.2 slice-start
  150.4 11.1 %all-to-all-start.1 = ((f32[4,1,8192]{2,1,0:T(1,128)}), f32[4,1,8192]{2,1,0:T(1,128)S(1)}, u32[]{:S(2)}, u32[]{:S(2)}) async-start(f32[4,1,8192]{2,1,0:T(1,128)} %broadcast_in_dim.127), calls=%async_computation.2 | async-start | bytes 262144 | tf_op jit(solution)/shard_map/all_to_all | solution.py:59
  163.3 23.4 %all-to-all-start.3 = ((bf16[64,16,256]{2,1,0:T(8,128)(2,1)}), bf16[64,16,256]{2,1,0:T(8,128)(2,1)S(1)}, u32[]{:S(2)}, u32[]{:S(2)}) async-start(bf16[64,16,256]{2,1,0:T(8,128)(2,1)} %bitcast.13), calls=%async_computation.4 | async-start | bytes 1048576 | tf_op jit(solution)/shard_map/all_to_all | solution.py:182
  186.7 6.7 %copy-start.5 = (f32[1,16,256]{2,1,0:T(8,128)S(1)}, f32[1,16,256]{2,1,0:T(8,128)}, u32[]{:S(2)}) copy-start(f32[1,16,256]{2,1,0:T(8,128)} %param.21) | copy-start | bytes 49156
  186.7 6.7 %copy-start.6 = (f32[1,16,256]{2,1,0:T(8,128)S(1)}, f32[1,16,256]{2,1,0:T(8,128)}, u32[]{:S(2)}) copy-start(f32[1,16,256]{2,1,0:T(8,128)} %param.24) | copy-start | bytes 49156
  186.7 6.7 %copy-start.7 = (f32[1,16,256]{2,1,0:T(8,128)S(1)}, f32[1,16,256]{2,1,0:T(8,128)}, u32[]{:S(2)}) copy-start(f32[1,16,256]{2,1,0:T(8,128)} %param.25) | copy-start | bytes 49156
  186.7 102.5 %all-to-all-start.2 = ((bf16[64,16,2048]{2,1,0:T(8,128)(2,1)}), bf16[64,16,2048]{2,1,0:T(8,128)(2,1)}, u32[]{:S(2)}, u32[]{:S(2)}) async-start(bf16[64,16,2048]{2,1,0:T(8,128)(2,1)} %bitcast.49), calls=%async_computation.3 | async-start | bytes 8388608 | tf_op jit(solution)/shard_map/all_to_all | solution.py:179
  198.8 93.2 %copy-start.1 = (f32[1,16,2048]{2,1,0:T(8,128)S(1)}, f32[1,16,2048]{2,1,0:T(8,128)}, u32[]{:S(2)}) copy-start(f32[1,16,2048]{2,1,0:T(8,128)} %param.20) | copy-start | bytes 393220
  198.8 93.2 %copy-start.3 = (f32[1,16,2048]{2,1,0:T(8,128)S(1)}, f32[1,16,2048]{2,1,0:T(8,128)}, u32[]{:S(2)}) copy-start(f32[1,16,2048]{2,1,0:T(8,128)} %param.22) | copy-start | bytes 393220
  198.8 93.2 %copy-start.4 = (f32[1,16,2048]{2,1,0:T(8,128)S(1)}, f32[1,16,2048]{2,1,0:T(8,128)}, u32[]{:S(2)}) copy-start(f32[1,16,2048]{2,1,0:T(8,128)} %param.23) | copy-start | bytes 393220
Sparse Core Ops, SparseCore 0:
  12.1 105.0 all-gather.1
Sparse Core Ops, SparseCore 1:
  143.7 46.9 reduce-scatter.1
